TPU v7x, 256 devices: a whole 4x4x8 slice. The times are simulated.
256 devices in a mesh: patch: 32 (over y, z), req: 4 (over x), owner: 2 (over core).
Axes of the slice: x: 4, y: 4, z: 8, core: 2. Of those that a mesh axis runs over, the one named last changes fastest.
Arguments:
- latents: bfloat16 [8, 256, 256, 320], P('req', 'patch', 'owner'), may hold values from -24 to 24
- timestep_embedding: bfloat16 [8, 1280], P('req'), may hold values from -6 to 6
- embedding_weight: bfloat16 [1280, 320], replicated, may hold values from -0.15625 to 0.15625
- group_norm_gain: float32 [2, 320], replicated, may hold values from 0.25 to 1.75
- group_norm_shift: float32 [2, 320], replicated, may hold values from -3 to 3
- kernel_weight: bfloat16 [2, 9, 320, 320], replicated, may hold values from -0.109375 to 0.109375
- plugin_reduce_library: bfloat16 [8, 2, 184320], P(('req', 'owner'), None, 'patch'), may hold values from -0.109375 to 0.109375
- plugin_expand_library: bfloat16 [8, 2, 20480], P(('req', 'owner'), None, 'patch'), may hold values from -0.75 to 0.75
- image_adapter: int32 [8, 1], P('req'), may hold values from 0 to 7
- adapter_bank_row: int32 [8], replicated, may hold values from 0 to 7, each once
Outputs:
- result: bfloat16 [8, 256, 256, 320], P('req', 'patch', 'owner')
Inputs may be any that keep to these rules, and one draw needn't show every extreme that they name: `image_adapter`: each image names one adapter; every adapter is named by some image. A permutation: adapter a is stored in bank row adapter_bank_row[a].
All inputs are finite; a program needn't handle non-finite values.
Results may differ from a plain program's by a relative error of at most 0.0055.
Values may be sent and summed in bfloat16 or wider, within the bound.
A program may use at most 128 MiB of HBM per device.

v0:
```python
import jax
import jax.numpy as jnp
from jax import lax
from jax.sharding import PartitionSpec as P

GROUPS = 32


def padded_2(block, sides, width):
    for axis, dim in sides:
        count = lax.axis_size(axis)
        forward = [(i, i + 1) for i in range(count - 1)]
        backward = [(target, source) for source, target in forward]
        low = lax.ppermute(
            lax.slice_in_dim(block, block.shape[dim] - width, None, axis=dim), axis, forward
        )
        high = lax.ppermute(lax.slice_in_dim(block, 0, width, axis=dim), axis, backward)
        block = jnp.concatenate([low, block, high], axis=dim)
    return block


def group_act(values, gain, shift):
    images, rows, columns, chans = values.shape
    grouped = values.reshape(images, rows, columns, GROUPS, chans // GROUPS)
    count = rows * columns * (chans // GROUPS) * lax.axis_size("patch") * lax.axis_size("owner")
    total = lax.psum(jnp.sum(grouped, axis=(1, 2, 4)), ("patch", "owner"))
    mean = total / count
    centered = grouped - mean[:, None, None, :, None]
    spread = lax.psum(jnp.sum(centered * centered, axis=(1, 2, 4)), ("patch", "owner"))
    var = spread / count
    normed = (centered / jnp.sqrt(var + 1e-05)[:, None, None, :, None]).reshape(values.shape)
    return jax.nn.silu(normed * gain + shift).astype(jnp.bfloat16)


def block_conv(act, kernel, reducing_filter, expanding_linear_map):
    images, rows, columns, chans = act.shape
    outward = kernel.shape[2]
    padded = padded_2(act, (("patch", 1), ("owner", 2)), 1)
    joined = jnp.concatenate(
        [jnp.broadcast_to(kernel[None], (images,) + kernel.shape), reducing_filter], axis=3
    )
    accum = jnp.zeros((images, rows, columns, joined.shape[3]), jnp.float32)
    for tap in range(9):
        row_off, col_off = divmod(tap, 3)
        window = padded[:, row_off : row_off + rows, col_off : col_off + columns, :]
        accum = accum + jnp.einsum(
            "bhwc,bcd->bhwd", window, joined[:, tap], preferred_element_type=jnp.float32
        )
    lowpart = accum[..., outward:].astype(jnp.bfloat16)
    return accum[..., :outward] + jnp.einsum(
        "bhwr,brd->bhwd", lowpart, expanding_linear_map, preferred_element_type=jnp.float32
    )


def local(
    latents,
    timestep_embedding,
    embedding_weight,
    group_norm_gain,
    group_norm_shift,
    kernel_weight,
    plugin_reduce_library,
    plugin_expand_library,
    image_adapter,
    adapter_bank_row,
):
    images, rows, columns, chans = latents.shape
    wanted = image_adapter[:, 0]
    table = jnp.arange(adapter_bank_row.shape[0], dtype=jnp.int32)
    slots = jnp.sum(
        jnp.where(wanted[:, None] == table[None, :], adapter_bank_row[None, :], 0), axis=1
    )
    full_down, full_up = (
        lax.all_gather(plugin_reduce_library, "patch", axis=2, tiled=True),
        lax.all_gather(plugin_expand_library, "patch", axis=2, tiled=True),
    )
    pieces = (
        lax.all_gather(full_down, ("req", "owner"), axis=0, tiled=True),
        lax.all_gather(full_up, ("req", "owner"), axis=0, tiled=True),
    )
    count = pieces[0].shape[0]
    match = (slots[:, None] == jnp.arange(count, dtype=jnp.int32)[None, :]).astype(jnp.bfloat16)
    first = jnp.einsum("ik,kjs->ijs", match, pieces[0], preferred_element_type=jnp.float32)
    second = jnp.einsum("ik,kjs->ijs", match, pieces[1], preferred_element_type=jnp.float32)
    down_sel = first.astype(jnp.bfloat16)
    up_sel = second.astype(jnp.bfloat16)
    rank = up_sel.shape[2] // chans
    down_all = down_sel.reshape(images, 2, 9, chans, rank)
    up_all = up_sel.reshape(images, 2, rank, chans)
    temb = jax.nn.silu(timestep_embedding.astype(jnp.float32)).astype(jnp.bfloat16)
    proj = jnp.dot(temb, embedding_weight, preferred_element_type=jnp.float32)
    source = latents.astype(jnp.float32)
    act1 = group_act(source, group_norm_gain[0], group_norm_shift[0])
    hidden1 = (
        block_conv(act1, kernel_weight[0], down_all[:, 0], up_all[:, 0]) + proj[:, None, None, :]
    ).astype(jnp.bfloat16)
    act2 = group_act(hidden1.astype(jnp.float32), group_norm_gain[1], group_norm_shift[1])
    result = source + block_conv(act2, kernel_weight[1], down_all[:, 1], up_all[:, 1])
    return result.astype(jnp.bfloat16)


def solution(mesh):
    in_specs = (
        P("req", "patch", "owner", None),
        P("req", None),
        P(),
        P(),
        P(),
        P(),
        P(("req", "owner"), None, "patch"),
        P(("req", "owner"), None, "patch"),
        P("req", None),
        P(),
    )
    out_specs = P("req", "patch", "owner", None)
    return jax.shard_map(local, mesh=mesh, in_specs=in_specs, out_specs=out_specs, check_vma=False)
```

profile of v0, /device:TPU:1, one launch (start us, length us, event | category | flops | bytes accessed | tf_op | source)
XLA Modules:
  0.0 778.4 jit_solution(10491722644223189108)
XLA Ops:
  6.6 47.2 %all_gather.12 = bf16[1,2,184320]{2,1,0:T(2,128)(2,1)} all-gather(bf16[1,2,5760]{2,1,0:T(2,128)(2,1)} %param.16), channel_id=1, replica_groups=mesh['patch'=32,'req'=4,'owner'=2] {'patch'}, dimensions={2}, use_global_device_ids=true | all-gather | bytes 760320 | tf_op jit(solution)/shard_map/all_gather | solution.py:74
  53.9 1.6 convert_reduce_fusion
  55.6 135.6 %psum.28 = f32[2,32]{1,0:T(2,128)S(1)} all-reduce(f32[2,32]{1,0:T(2,128)S(1)} %reduce_sum.59), channel_id=1, replica_groups=mesh['patch'=32,'req'=4,'owner'=2] {'patch','owner'}, use_global_device_ids=true, to_apply=%region_2.3 | all-reduce | flops 64 | bytes 512 | tf_op jit(solution)/shard_map/psum | solution.py:26
  192.2 124.0 %psum.29 = f32[2,32]{1,0:T(2,128)S(1)} all-reduce(f32[2,32]{1,0:T(2,128)S(1)} %reduce_sum.62), channel_id=1, replica_groups=mesh['patch'=32,'req'=4,'owner'=2] {'patch','owner'}, use_global_device_ids=true, to_apply=%region_5.6 | all-reduce | flops 64 | bytes 512 | tf_op jit(solution)/shard_map/psum | solution.py:29
  316.5 1.4 multiply_convert_fusion.1
  320.5 32.0 %all_gather.14 = bf16[1,2,20480]{2,1,0:T(2,128)(2,1)S(1)} all-gather(bf16[1,2,640]{2,1,0:T(2,128)(2,1)S(1)} %copy-done.16), channel_id=1, replica_groups=mesh['patch'=32,'req'=4,'owner'=2] {'patch'}, dimensions={2}, use_global_device_ids=true | all-gather | bytes 84480 | tf_op jit(solution)/shard_map/all_gather | solution.py:75
  352.5 24.4 %all_gather.15 = bf16[8,2,20480]{2,1,0:T(2,128)(2,1)S(1)} all-gather(bf16[1,2,20480]{2,1,0:T(2,128)(2,1)S(1)} %all_gather.14), channel_id=1, replica_groups=mesh['patch'=32,'req'=4,'owner'=2] {'req','owner'}, dimensions={0}, use_global_device_ids=true | all-gather | bytes 737280 | tf_op jit(solution)/shard_map/all_gather | solution.py:79
  377.0 4.8 slice_bitcast_fusion
  382.5 2.5 fusion.147
  385.0 1.9 copy.87
  388.2 1.9 copy.94
  390.1 3.5 collective-permute-start.3
  394.7 1.7 copy.88
  396.3 1.6 copy.95
  398.0 5.7 pad_maximum_fusion
  403.7 10.7 %convolution_convert_fusion = bf16[2,2,184320]{2,0,1:T(2,128)(2,1)} fusion(bf16[8,2,184320]{2,1,0:T(2,128)(2,1)} %all-gather.2.cloned.1.call-done, s32[2]{0:T(128)S(1)} %fusion.123), kind=kOutput, calls=%fused_computation | convolution fusion | flops 12533776 | bytes 7372808 | tf_op jit(solution)/shard_map/ik,kjs->ijs/dot_general | solution.py:83
  414.4 4.7 reshape.54
  419.1 3.3 fusion.145
  425.4 2.7 fusion.52
  428.2 2.9 fusion.54
  431.1 2.9 fusion.50
  434.0 2.7 fusion.48
  436.7 2.7 fusion.80
  439.4 2.7 fusion.14
  442.2 2.7 fusion.18
  444.9 9.6 %add_add_fusion.1 = f32[2,8,128,384]{2,3,1,0:T(8,128)} fusion(f32[2,8,128,384]{2,3,1,0:T(8,128)} %fusion.18, f32[2,8,128,384]{2,3,1,0:T(8,128)} %fusion.48, f32[2,8,128,384]{2,3,1,0:T(8,128)} %fusion.50, f32[2,8,128,384]{2,3,1,0:T(8,128)} %fusion.80, f32[2,8,128,384]{2,3,1,0:T(8,128)S(1)} %copy-done.10, f32[2,8,128,384]{2,3,1,0:T(8,128)} %fusion.54, ...), kind=kOutput, calls=%fused_computation.45 | convolution fusion | flops 510590976 | bytes 35520512 | tf_op jit(solution)/shard_map/bhwc,bcd->bhwd/dot_general | solution.py:46
  454.5 2.6 convert_reduce_fusion.1
  457.3 122.8 %psum.30 = f32[2,32]{1,0:T(2,128)S(1)} all-reduce(f32[2,32]{1,0:T(2,128)S(1)} %reduce_sum.82), channel_id=1, replica_groups=mesh['patch'=32,'req'=4,'owner'=2] {'patch','owner'}, use_global_device_ids=true, to_apply=%region_9.10 | all-reduce | flops 64 | bytes 512 | tf_op jit(solution)/shard_map/psum | solution.py:26
  581.0 127.5 %psum.31 = f32[2,32]{1,0:T(2,128)S(1)} all-reduce(f32[2,32]{1,0:T(2,128)S(1)} %reduce_sum.85), channel_id=1, replica_groups=mesh['patch'=32,'req'=4,'owner'=2] {'patch','owner'}, use_global_device_ids=true, to_apply=%region_12.13 | all-reduce | flops 64 | bytes 512 | tf_op jit(solution)/shard_map/psum | solution.py:29
  711.5 1.5 copy.166
  714.9 3.2 fusion.97
  718.1 1.8 collective-permute-done.5
  720.1 2.4 fusion.146
  722.5 1.9 copy.104
  725.7 1.9 copy.109
  727.7 3.7 collective-permute-start.7
  731.4 4.1 fusion.22
  735.5 2.7 fusion.26
  738.2 1.9 copy.105
  740.1 1.6 copy.110
  741.8 5.0 pad_maximum_fusion.1
  746.8 2.7 fusion.42
  749.5 2.7 fusion.38
  752.2 2.9 fusion.40
  755.1 2.9 fusion.36
  758.0 2.7 fusion.34
  760.7 8.9 %add_add_fusion = f32[2,8,128,384]{2,3,1,0:T(8,128)S(1)} fusion(f32[2,8,128,384]{2,3,1,0:T(8,128)} %fusion.26, f32[2,8,128,384]{2,3,1,0:T(8,128)} %fusion.34, f32[2,8,128,384]{2,3,1,0:T(8,128)} %fusion.36, f32[2,8,128,384]{2,3,1,0:T(8,128)S(1)} %copy-done.9, f32[2,8,128,384]{2,3,1,0:T(8,128)} %fusion.38, f32[2,8,128,384]{2,3,1,0:T(8,128)} %fusion.40, ...), kind=kOutput, calls=%fused_computation.44 | convolution fusion | flops 510590976 | bytes 35520512 | tf_op jit(solution)/shard_map/bhwc,bcd->bhwd/dot_general | solution.py:46
  769.6 1.6 fusion.11
  (100 shorter events, 17.5 us)
Async XLA Ops:
  6.5 375.3 %copy-start = (bf16[1280,320]{0,1:T(8,128)(2,1)S(1)}, bf16[1280,320]{0,1:T(8,128)(2,1)}, u32[]{:S(2)}) copy-start(bf16[1280,320]{0,1:T(8,128)(2,1)} %param.12) | copy-start | bytes 2457604
  6.5 184.9 %copy-start.5 = (bf16[2,8,128,320]{2,3,1,0:T(8,128)(2,1)S(1)}, bf16[2,8,128,320]{2,3,1,0:T(8,128)(2,1)}, u32[]{:S(2)}) copy-start(bf16[2,8,128,320]{2,3,1,0:T(8,128)(2,1)} %param.10) | copy-start | bytes 3932164
  6.5 309.9 %copy-start.15 = (f32[2,320]{1,0:T(2,128)S(1)}, f32[2,320]{1,0:T(2,128)}, u32[]{:S(2)}) copy-start(f32[2,320]{1,0:T(2,128)} %param.13) | copy-start | bytes 7684
  6.5 309.9 %copy-start.14 = (f32[2,320]{1,0:T(2,128)S(1)}, f32[2,320]{1,0:T(2,128)}, u32[]{:S(2)}) copy-start(f32[2,320]{1,0:T(2,128)} %param.14) | copy-start | bytes 7684
  6.5 397.2 %all-gather.2.cloned.1.call-start = ((), (), s32[]{:S(2)}) async-start(), calls=%async_computation | async-start | bytes 6635520 | tf_op jit(solution)/shard_map/all_gather | solution.py:78
  53.8 266.6 %copy-start.16 = (bf16[1,2,640]{2,1,0:T(2,128)(2,1)S(1)}, bf16[1,2,640]{2,1,0:T(2,128)(2,1)}, u32[]{:S(2)}) copy-start(bf16[1,2,640]{2,1,0:T(2,128)(2,1)} %param.17) | copy-start | bytes 7684
  317.9 64.4 %collective-permute-start = (bf16[2,1,128,320]{2,3,1,0:T(8,128)(2,1)S(1)}, bf16[2,1,128,320]{2,3,1,0:T(8,128)(2,1)S(1)}, u32[]{:S(2)}, u32[]{:S(2)}) collective-permute-start(bf16[2,1,128,320]{2,3,1,0:T(8,128)(2,1)S(1)} %get-tuple-element.23), channel_id=1, source_target_pairs={{0,8},{8,16},{16,24},{24,32},{32,40},{40,48},{48,56},{56,64},{64,7... | collective-permute-start | bytes 491528 | tf_op jit(solution)/shard_map/ppermute | solution.py:14
  319.2 63.1 %collective-permute-start.1 = (bf16[2,1,128,320]{2,3,1,0:T(8,128)(2,1)S(1)}, bf16[2,1,128,320]{2,3,1,0:T(8,128)(2,1)S(1)}, u32[]{:S(2)}, u32[]{:S(2)}) collective-permute-start(bf16[2,1,128,320]{2,3,1,0:T(8,128)(2,1)S(1)} %get-tuple-element.24), channel_id=1, source_target_pairs={{8,0},{16,8},{24,16},{32,24},{40,32},{48,40},{56,48},{64,56},{72,6... | collective-permute-start | bytes 491528 | tf_op jit(solution)/shard_map/ppermute | solution.py:17
  377.0 4.8 copy-start.13
  377.0 5.1 copy-start.17
  377.0 5.1 copy-start.18
  386.9 7.8 collective-permute-start.2
  390.1 6.3 collective-permute-start.3
  419.1 3.4 copy-start.12
  422.5 1.9 copy-start.8
  425.4 2.7 copy-start.7
  442.2 2.7 copy-start.10
  708.7 5.5 copy-start.11
  710.1 9.8 %copy-start.3 = (bf16[2,8,128,320]{2,3,1,0:T(8,128)(2,1)}, bf16[2,8,128,320]{2,3,1,0:T(8,128)(2,1)S(1)}, u32[]{:S(2)}) copy-start(bf16[2,8,128,320]{2,3,1,0:T(8,128)(2,1)S(1)} %multiply_convert_fusion) | copy-start | bytes 3932164
  710.2 7.9 %collective-permute-start.4 = (bf16[2,1,128,320]{2,3,1,0:T(8,128)(2,1)S(1)}, bf16[2,1,128,320]{2,3,1,0:T(8,128)(2,1)S(1)}, u32[]{:S(2)}, u32[]{:S(2)}) collective-permute-start(bf16[2,1,128,320]{2,3,1,0:T(8,128)(2,1)S(1)} %get-tuple-element.21), channel_id=1, source_target_pairs={{0,8},{8,16},{16,24},{24,32},{32,40},{40,48},{48,56},{56,64},{64,7... | collective-permute-start | bytes 491528 | tf_op jit(solution)/shard_map/ppermute | solution.py:14
  712.9 7.0 collective-permute-start.5
  714.8 3.2 copy-start.2
  724.4 13.8 %collective-permute-start.6 = (bf16[2,10,1,320]{3,0,2,1:T(2,128)(2,1)S(1)}, bf16[2,10,1,320]{3,0,2,1:T(2,128)(2,1)S(1)}, u32[]{:S(2)}, u32[]{:S(2)}) collective-permute-start(bf16[2,10,1,320]{3,0,2,1:T(2,128)(2,1)S(1)} %copy.104), channel_id=1, source_target_pairs={{0,1},{2,3},{4,5},{6,7},{8,9},{10,11},{12,13},{14,15},{16,17},{18,... | collective-permute-start | bytes 38408 | tf_op jit(solution)/shard_map/ppermute | solution.py:14
  725.7 9.8 %slice-start = ((s8[4423680]{0:T(1024)(128)(4,1)}), s8[229376]{0:T(1024)(128)(4,1)S(1)}, s32[]{:S(2)}) async-start(s8[4423680]{0:T(1024)(128)(4,1)} %bitcast.145), calls=%async_computation.1 | async-start | bytes 458752
  727.7 7.8 %slice-start.1 = ((s8[4423680]{0:T(1024)(128)(4,1)}), s8[4194304]{0:T(1024)(128)(4,1)S(1)}, s32[]{:S(2)}) async-start(s8[4423680]{0:T(1024)(128)(4,1)} %bitcast.145), calls=%async_computation.2 | async-start | bytes 8388608
  727.7 7.8 %copy-start.4 = (bf16[2,8,128,320]{2,3,1,0:T(8,128)(2,1)S(1)}, bf16[2,8,128,320]{2,3,1,0:T(8,128)(2,1)}, u32[]{:S(2)}) copy-start(bf16[2,8,128,320]{2,3,1,0:T(8,128)(2,1)} %copy-done.3) | copy-start | bytes 3932164
  727.7 12.5 %collective-permute-start.7 = (bf16[2,10,1,320]{3,0,2,1:T(2,128)(2,1)S(1)}, bf16[2,10,1,320]{3,0,2,1:T(2,128)(2,1)S(1)}, u32[]{:S(2)}, u32[]{:S(2)}) collective-permute-start(bf16[2,10,1,320]{3,0,2,1:T(2,128)(2,1)S(1)} %copy.109), channel_id=1, source_target_pairs={{1,0},{3,2},{5,4},{7,6},{9,8},{11,10},{13,12},{15,14},{17,16},{19,... | collective-permute-start | bytes 38408 | tf_op jit(solution)/shard_map/ppermute | solution.py:17
  740.1 6.7 slice-start.2
  741.8 5.0 slice-start.3
  758.0 2.7 copy-start.9
  760.7 8.9 %copy-start.6 = (bf16[2,8,128,320]{2,3,1,0:T(8,128)(2,1)S(1)}, bf16[2,8,128,320]{2,3,1,0:T(8,128)(2,1)}, u32[]{:S(2)}) copy-start(bf16[2,8,128,320]{2,3,1,0:T(8,128)(2,1)} %param.10) | copy-start | bytes 3932164
  760.7 10.6 %copy-start.1 = (bf16[1280,320]{0,1:T(8,128)(2,1)S(1)}, bf16[1280,320]{0,1:T(8,128)(2,1)}, u32[]{:S(2)}) copy-start(bf16[1280,320]{0,1:T(8,128)(2,1)} %param.12) | copy-start | bytes 2457604
Sparse Core Ops, SparseCore 0:
  54.0 51.1 all-gather.1
where the time goes:
time: 784 us; the launch traced here: 778 us
  blocking collectives  614 us (78%)
  matrix products  79 us (10%)
  local copies, waits for them, and re-layouts  37.7 us (5%)
  other arithmetic  17 us (2%)
  starting transfers between devices  15 us (2%)
  between operations  14.1 us (2%)
    psum x2, blocking collectives, group_act(): total = lax.psum(jnp.sum(grouped, axis=(1, 2, 4)), ('patch', 'owner'))  258 us
    psum x2, blocking collectives, group_act(): lax.psum(jnp.sum(centered * centered, axis=(1, 2, 4)), ('patch', 'owner'))  252 us
    dot_general x18, matrix products, block_conv(): jnp.einsum('bhwc,bcd->bhwd', window, joined[:, tap], preferred_element_ty...  62.9 us
    all_gather x1, blocking collectives, local(): lax.all_gather(plugin_reduce_library, 'patch', axis=2, tiled=True)  47.2 us
    all_gather x1, blocking collectives, local(): lax.all_gather(plugin_expand_library, 'patch', axis=2, tiled=True)  32 us
    all_gather x1, blocking collectives, local(): lax.all_gather(full_up, ('req', 'owner'), axis=0, tiled=True)  24.4 us
  transfers between devices with their start and end apart: 9, of which 1 were waited for; matrix products, arithmetic and copies ran while one was open for 5% of the time, Pallas kernels for 0%

commit v1 on v0

--- a/solution.py
+++ b/solution.py
@@ -23,7 +23,7 @@
     images, rows, columns, chans = values.shape
     grouped = values.reshape(images, rows, columns, GROUPS, chans // GROUPS)
     count = rows * columns * (chans // GROUPS) * lax.axis_size("patch") * lax.axis_size("owner")
-    total = lax.psum(jnp.sum(grouped, axis=(1, 2, 4)), ("patch", "owner"))
+    total = lax.psum(lax.psum(jnp.sum(grouped, axis=(1, 2, 4)), "patch"), "owner")
     mean = total / count
     centered = grouped - mean[:, None, None, :, None]
     spread = lax.psum(jnp.sum(centered * centered, axis=(1, 2, 4)), ("patch", "owner"))

time: 784 us -> 682 us (0.87)
  blocking collectives: 614 us -> 512 us
    psum x2 -> x4, blocking collectives: 258 us -> 160 us  [the longest x2 117 us: group_act(): lax.psum(jnp.sum(grouped, axis=(1, 2, 4)), 'patch')]
  transfers between devices with their start and end apart: 9 -> 9, of which waited for: 1 -> 1; matrix products, arithmetic and copies ran while one was open for 5% -> 6% of each run, Pallas kernels for 0% -> 0%
where the time goes in v1:
time: 682 us; the launch traced here: 677 us
  blocking collectives  512 us (75%)
  matrix products  79 us (12%)
  local copies, waits for them, and re-layouts  37.7 us (6%)
  other arithmetic  17 us (2%)
  starting transfers between devices  15.2 us (2%)
  between operations  14.1 us (2%)
    psum x2, blocking collectives, group_act(): lax.psum(jnp.sum(centered * centered, axis=(1, 2, 4)), ('patch', 'owner'))  248 us
    psum x2, blocking collectives, group_act(): lax.psum(jnp.sum(grouped, axis=(1, 2, 4)), 'patch')  117 us
    dot_general x18, matrix products, block_conv(): jnp.einsum('bhwc,bcd->bhwd', window, joined[:, tap], preferred_element_ty...  62.9 us
    all_gather x1, blocking collectives, local(): lax.all_gather(plugin_reduce_library, 'patch', axis=2, tiled=True)  47.2 us
    psum x2, blocking collectives, group_act(): lax.psum(lax.psum(jnp.sum(grouped, axis=(1, 2, 4)), 'patch'), 'owner')  43.8 us
    all_gather x1, blocking collectives, local(): lax.all_gather(plugin_expand_library, 'patch', axis=2, tiled=True)  32 us
    all_gather x1, blocking collectives, local(): lax.all_gather(full_up, ('req', 'owner'), axis=0, tiled=True)  24.6 us
  transfers between devices with their start and end apart: 9, of which 1 were waited for; matrix products, arithmetic and copies ran while one was open for 6% of the time, Pallas kernels for 0%

profile of v1, /device:TPU:1, one launch (start us, length us, event | category | flops | bytes accessed | tf_op | source)
XLA Modules:
  0.0 676.6 jit_solution(5969306463648355335)
XLA Ops:
  6.6 47.2 %all_gather.12 = bf16[1,2,184320]{2,1,0:T(2,128)(2,1)} all-gather(bf16[1,2,5760]{2,1,0:T(2,128)(2,1)} %param.16), channel_id=1, replica_groups=mesh['patch'=32,'req'=4,'owner'=2] {'patch'}, dimensions={2}, use_global_device_ids=true | all-gather | bytes 760320 | tf_op jit(solution)/shard_map/all_gather | solution.py:74
  53.9 1.6 convert_reduce_fusion
  55.6 58.1 %psum.42 = f32[2,32]{1,0:T(2,128)S(1)} all-reduce(f32[2,32]{1,0:T(2,128)S(1)} %reduce_sum.59), channel_id=1, replica_groups=mesh['patch'=32,'req'=4,'owner'=2] {'patch'}, use_global_device_ids=true, to_apply=%region_2.3 | all-reduce | flops 64 | bytes 512 | tf_op jit(solution)/shard_map/psum | solution.py:26
  113.7 28.6 %psum.43 = f32[2,32]{1,0:T(2,128)S(1)} all-reduce(f32[2,32]{1,0:T(2,128)S(1)} %psum.42), channel_id=1, replica_groups=mesh['patch'=32,'req'=4,'owner'=2] {'owner'}, use_global_device_ids=true, to_apply=%region_3.4 | all-reduce | flops 64 | bytes 512 | tf_op jit(solution)/shard_map/psum | solution.py:26
  143.3 123.7 %psum.44 = f32[2,32]{1,0:T(2,128)S(1)} all-reduce(f32[2,32]{1,0:T(2,128)S(1)} %reduce_sum.62), channel_id=1, replica_groups=mesh['patch'=32,'req'=4,'owner'=2] {'patch','owner'}, use_global_device_ids=true, to_apply=%region_6.7 | all-reduce | flops 64 | bytes 512 | tf_op jit(solution)/shard_map/psum | solution.py:29
  271.3 32.0 %all_gather.14 = bf16[1,2,20480]{2,1,0:T(2,128)(2,1)S(1)} all-gather(bf16[1,2,640]{2,1,0:T(2,128)(2,1)S(1)} %copy-done.16), channel_id=1, replica_groups=mesh['patch'=32,'req'=4,'owner'=2] {'patch'}, dimensions={2}, use_global_device_ids=true | all-gather | bytes 84480 | tf_op jit(solution)/shard_map/all_gather | solution.py:75
  303.3 24.6 %all_gather.15 = bf16[8,2,20480]{2,1,0:T(2,128)(2,1)S(1)} all-gather(bf16[1,2,20480]{2,1,0:T(2,128)(2,1)S(1)} %all_gather.14), channel_id=1, replica_groups=mesh['patch'=32,'req'=4,'owner'=2] {'req','owner'}, dimensions={0}, use_global_device_ids=true | all-gather | bytes 737280 | tf_op jit(solution)/shard_map/all_gather | solution.py:79
  327.9 4.8 slice_bitcast_fusion
  333.5 2.5 fusion.147
  336.0 1.9 copy.87
  339.1 1.9 copy.94
  341.0 3.5 collective-permute-start.3
  345.6 1.7 copy.88
  347.3 1.6 copy.95
  348.9 5.7 pad_maximum_fusion
  354.7 10.7 %convolution_convert_fusion = bf16[2,2,184320]{2,0,1:T(2,128)(2,1)} fusion(bf16[8,2,184320]{2,1,0:T(2,128)(2,1)} %all-gather.2.cloned.1.call-done, s32[2]{0:T(128)S(1)} %fusion.123), kind=kOutput, calls=%fused_computation | convolution fusion | flops 12533776 | bytes 7372808 | tf_op jit(solution)/shard_map/ik,kjs->ijs/dot_general | solution.py:83
  365.4 4.7 reshape.54
  370.0 3.3 fusion.145
  376.4 2.7 fusion.52
  379.1 2.9 fusion.54
  382.0 2.9 fusion.50
  384.9 2.7 fusion.48
  387.7 2.7 fusion.80
  390.4 2.7 fusion.14
  393.1 2.7 fusion.18
  395.8 9.6 %add_add_fusion.1 = f32[2,8,128,384]{2,3,1,0:T(8,128)} fusion(f32[2,8,128,384]{2,3,1,0:T(8,128)} %fusion.18, f32[2,8,128,384]{2,3,1,0:T(8,128)} %fusion.48, f32[2,8,128,384]{2,3,1,0:T(8,128)} %fusion.50, f32[2,8,128,384]{2,3,1,0:T(8,128)} %fusion.80, f32[2,8,128,384]{2,3,1,0:T(8,128)S(1)} %copy-done.10, f32[2,8,128,384]{2,3,1,0:T(8,128)} %fusion.54, ...), kind=kOutput, calls=%fused_computation.45 | convolution fusion | flops 510590976 | bytes 35520512 | tf_op jit(solution)/shard_map/bhwc,bcd->bhwd/dot_general | solution.py:46
  405.5 2.6 convert_reduce_fusion.1
  408.3 58.5 %psum.45 = f32[2,32]{1,0:T(2,128)S(1)} all-reduce(f32[2,32]{1,0:T(2,128)S(1)} %reduce_sum.82), channel_id=1, replica_groups=mesh['patch'=32,'req'=4,'owner'=2] {'patch'}, use_global_device_ids=true, to_apply=%region_10.11 | all-reduce | flops 64 | bytes 512 | tf_op jit(solution)/shard_map/psum | solution.py:26
  466.8 15.1 %psum.46 = f32[2,32]{1,0:T(2,128)S(1)} all-reduce(f32[2,32]{1,0:T(2,128)S(1)} %psum.45), channel_id=1, replica_groups=mesh['patch'=32,'req'=4,'owner'=2] {'owner'}, use_global_device_ids=true, to_apply=%region_11.12 | all-reduce | flops 64 | bytes 512 | tf_op jit(solution)/shard_map/psum | solution.py:26
  482.8 123.9 %psum.47 = f32[2,32]{1,0:T(2,128)S(1)} all-reduce(f32[2,32]{1,0:T(2,128)S(1)} %reduce_sum.85), channel_id=1, replica_groups=mesh['patch'=32,'req'=4,'owner'=2] {'patch','owner'}, use_global_device_ids=true, to_apply=%region_14.15 | all-reduce | flops 64 | bytes 512 | tf_op jit(solution)/shard_map/psum | solution.py:29
  613.1 3.2 fusion.97
  616.3 1.7 collective-permute-done.5
  618.2 2.4 fusion.146
  620.6 1.9 copy.104
  623.8 1.9 copy.109
  625.7 3.9 collective-permute-start.7
  629.6 4.1 fusion.22
  633.7 2.7 fusion.26
  636.5 1.9 copy.105
  638.3 1.6 copy.110
  640.0 5.0 pad_maximum_fusion.1
  645.0 2.7 fusion.42
  647.7 2.7 fusion.38
  650.4 2.9 fusion.40
  653.3 2.9 fusion.36
  656.2 2.7 fusion.34
  658.9 8.9 %add_add_fusion = f32[2,8,128,384]{2,3,1,0:T(8,128)S(1)} fusion(f32[2,8,128,384]{2,3,1,0:T(8,128)} %fusion.26, f32[2,8,128,384]{2,3,1,0:T(8,128)} %fusion.34, f32[2,8,128,384]{2,3,1,0:T(8,128)} %fusion.36, f32[2,8,128,384]{2,3,1,0:T(8,128)S(1)} %copy-done.9, f32[2,8,128,384]{2,3,1,0:T(8,128)} %fusion.38, f32[2,8,128,384]{2,3,1,0:T(8,128)} %fusion.40, ...), kind=kOutput, calls=%fused_computation.44 | convolution fusion | flops 510590976 | bytes 35520512 | tf_op jit(solution)/shard_map/bhwc,bcd->bhwd/dot_general | solution.py:46
  667.8 1.6 fusion.11
  (102 shorter events, 20.3 us)
Async XLA Ops:
  6.5 326.2 %copy-start = (bf16[1280,320]{0,1:T(8,128)(2,1)S(1)}, bf16[1280,320]{0,1:T(8,128)(2,1)}, u32[]{:S(2)}) copy-start(bf16[1280,320]{0,1:T(8,128)(2,1)} %param.12) | copy-start | bytes 2457604
  6.5 136.0 %copy-start.5 = (bf16[2,8,128,320]{2,3,1,0:T(8,128)(2,1)S(1)}, bf16[2,8,128,320]{2,3,1,0:T(8,128)(2,1)}, u32[]{:S(2)}) copy-start(bf16[2,8,128,320]{2,3,1,0:T(8,128)(2,1)} %param.10) | copy-start | bytes 3932164
  6.5 260.7 %copy-start.15 = (f32[2,320]{1,0:T(2,128)S(1)}, f32[2,320]{1,0:T(2,128)}, u32[]{:S(2)}) copy-start(f32[2,320]{1,0:T(2,128)} %param.13) | copy-start | bytes 7684
  6.5 260.7 %copy-start.14 = (f32[2,320]{1,0:T(2,128)S(1)}, f32[2,320]{1,0:T(2,128)}, u32[]{:S(2)}) copy-start(f32[2,320]{1,0:T(2,128)} %param.14) | copy-start | bytes 7684
  6.5 348.1 %all-gather.2.cloned.1.call-start = ((), (), s32[]{:S(2)}) async-start(), calls=%async_computation | async-start | bytes 6635520 | tf_op jit(solution)/shard_map/all_gather | solution.py:78
  53.8 217.4 %copy-start.16 = (bf16[1,2,640]{2,1,0:T(2,128)(2,1)S(1)}, bf16[1,2,640]{2,1,0:T(2,128)(2,1)}, u32[]{:S(2)}) copy-start(bf16[1,2,640]{2,1,0:T(2,128)(2,1)} %param.17) | copy-start | bytes 7684
  268.7 64.6 %collective-permute-start = (bf16[2,1,128,320]{2,3,1,0:T(8,128)(2,1)S(1)}, bf16[2,1,128,320]{2,3,1,0:T(8,128)(2,1)S(1)}, u32[]{:S(2)}, u32[]{:S(2)}) collective-permute-start(bf16[2,1,128,320]{2,3,1,0:T(8,128)(2,1)S(1)} %get-tuple-element.23), channel_id=1, source_target_pairs={{0,8},{8,16},{16,24},{24,32},{32,40},{40,48},{48,56},{56,64},{64,7... | collective-permute-start | bytes 491528 | tf_op jit(solution)/shard_map/ppermute | solution.py:14
  270.0 63.3 %collective-permute-start.1 = (bf16[2,1,128,320]{2,3,1,0:T(8,128)(2,1)S(1)}, bf16[2,1,128,320]{2,3,1,0:T(8,128)(2,1)S(1)}, u32[]{:S(2)}, u32[]{:S(2)}) collective-permute-start(bf16[2,1,128,320]{2,3,1,0:T(8,128)(2,1)S(1)} %get-tuple-element.24), channel_id=1, source_target_pairs={{8,0},{16,8},{24,16},{32,24},{40,32},{48,40},{56,48},{64,56},{72,6... | collective-permute-start | bytes 491528 | tf_op jit(solution)/shard_map/ppermute | solution.py:17
  327.9 4.8 copy-start.13
  327.9 5.1 copy-start.17
  327.9 5.1 copy-start.18
  337.8 7.8 %collective-permute-start.2 = (bf16[2,10,1,320]{3,0,2,1:T(2,128)(2,1)S(1)}, bf16[2,10,1,320]{3,0,2,1:T(2,128)(2,1)S(1)}, u32[]{:S(2)}, u32[]{:S(2)}) collective-permute-start(bf16[2,10,1,320]{3,0,2,1:T(2,128)(2,1)S(1)} %copy.87), channel_id=1, source_target_pairs={{0,1},{2,3},{4,5},{6,7},{8,9},{10,11},{12,13},{14,15},{16,17},{18,... | collective-permute-start | bytes 38408 | tf_op jit(solution)/shard_map/ppermute | solution.py:14
  341.0 6.3 collective-permute-start.3
  370.0 3.4 copy-start.12
  373.4 1.9 copy-start.8
  376.4 2.7 copy-start.7
  393.1 2.7 copy-start.10
  606.9 5.5 copy-start.11
  608.3 9.6 %copy-start.3 = (bf16[2,8,128,320]{2,3,1,0:T(8,128)(2,1)}, bf16[2,8,128,320]{2,3,1,0:T(8,128)(2,1)S(1)}, u32[]{:S(2)}) copy-start(bf16[2,8,128,320]{2,3,1,0:T(8,128)(2,1)S(1)} %multiply_convert_fusion) | copy-start | bytes 3932164
  608.4 7.9 %collective-permute-start.4 = (bf16[2,1,128,320]{2,3,1,0:T(8,128)(2,1)S(1)}, bf16[2,1,128,320]{2,3,1,0:T(8,128)(2,1)S(1)}, u32[]{:S(2)}, u32[]{:S(2)}) collective-permute-start(bf16[2,1,128,320]{2,3,1,0:T(8,128)(2,1)S(1)} %get-tuple-element.21), channel_id=1, source_target_pairs={{0,8},{8,16},{16,24},{24,32},{32,40},{40,48},{48,56},{56,64},{64,7... | collective-permute-start | bytes 491528 | tf_op jit(solution)/shard_map/ppermute | solution.py:14
  611.2 6.8 %collective-permute-start.5 = (bf16[2,1,128,320]{2,3,1,0:T(8,128)(2,1)S(1)}, bf16[2,1,128,320]{2,3,1,0:T(8,128)(2,1)S(1)}, u32[]{:S(2)}, u32[]{:S(2)}) collective-permute-start(bf16[2,1,128,320]{2,3,1,0:T(8,128)(2,1)S(1)} %get-tuple-element.22), channel_id=1, source_target_pairs={{8,0},{16,8},{24,16},{32,24},{40,32},{48,40},{56,48},{64,56},{72,6... | collective-permute-start | bytes 491528 | tf_op jit(solution)/shard_map/ppermute | solution.py:17
  613.1 3.2 copy-start.2
  622.5 14.0 %collective-permute-start.6 = (bf16[2,10,1,320]{3,0,2,1:T(2,128)(2,1)S(1)}, bf16[2,10,1,320]{3,0,2,1:T(2,128)(2,1)S(1)}, u32[]{:S(2)}, u32[]{:S(2)}) collective-permute-start(bf16[2,10,1,320]{3,0,2,1:T(2,128)(2,1)S(1)} %copy.104), channel_id=1, source_target_pairs={{0,1},{2,3},{4,5},{6,7},{8,9},{10,11},{12,13},{14,15},{16,17},{18,... | collective-permute-start | bytes 38408 | tf_op jit(solution)/shard_map/ppermute | solution.py:14
  623.8 9.9 %slice-start = ((s8[4423680]{0:T(1024)(128)(4,1)}), s8[229376]{0:T(1024)(128)(4,1)S(1)}, s32[]{:S(2)}) async-start(s8[4423680]{0:T(1024)(128)(4,1)} %bitcast.145), calls=%async_computation.1 | async-start | bytes 458752
  625.7 8.0 %slice-start.1 = ((s8[4423680]{0:T(1024)(128)(4,1)}), s8[4194304]{0:T(1024)(128)(4,1)S(1)}, s32[]{:S(2)}) async-start(s8[4423680]{0:T(1024)(128)(4,1)} %bitcast.145), calls=%async_computation.2 | async-start | bytes 8388608
  625.7 8.0 %copy-start.4 = (bf16[2,8,128,320]{2,3,1,0:T(8,128)(2,1)S(1)}, bf16[2,8,128,320]{2,3,1,0:T(8,128)(2,1)}, u32[]{:S(2)}) copy-start(bf16[2,8,128,320]{2,3,1,0:T(8,128)(2,1)} %copy-done.3) | copy-start | bytes 3932164
  625.7 12.6 %collective-permute-start.7 = (bf16[2,10,1,320]{3,0,2,1:T(2,128)(2,1)S(1)}, bf16[2,10,1,320]{3,0,2,1:T(2,128)(2,1)S(1)}, u32[]{:S(2)}, u32[]{:S(2)}) collective-permute-start(bf16[2,10,1,320]{3,0,2,1:T(2,128)(2,1)S(1)} %copy.109), channel_id=1, source_target_pairs={{1,0},{3,2},{5,4},{7,6},{9,8},{11,10},{13,12},{15,14},{17,16},{19,... | collective-permute-start | bytes 38408 | tf_op jit(solution)/shard_map/ppermute | solution.py:17
  638.3 6.7 slice-start.2
  640.0 5.0 slice-start.3
  656.2 2.7 copy-start.9
  658.9 8.9 %copy-start.6 = (bf16[2,8,128,320]{2,3,1,0:T(8,128)(2,1)S(1)}, bf16[2,8,128,320]{2,3,1,0:T(8,128)(2,1)}, u32[]{:S(2)}) copy-start(bf16[2,8,128,320]{2,3,1,0:T(8,128)(2,1)} %param.10) | copy-start | bytes 3932164
  658.9 10.5 %copy-start.1 = (bf16[1280,320]{0,1:T(8,128)(2,1)S(1)}, bf16[1280,320]{0,1:T(8,128)(2,1)}, u32[]{:S(2)}) copy-start(bf16[1280,320]{0,1:T(8,128)(2,1)} %param.12) | copy-start | bytes 2457604
Sparse Core Ops, SparseCore 0:
  54.0 51.1 all-gather.1
